TPU v7x, 512 devices: a whole 4x4x16 slice. The times are simulated.
512 devices in a mesh: gx: 16 (over x, z_hi, core), gy: 32 (over z_lo, y).
Axes of the slice: x: 4, y: 4, z: 16 (z_hi: 2, z_lo: 8; z = z_hi * 8 + z_lo), core: 2. Of those that a mesh axis runs over, the one named last changes fastest.
Arguments:
- fine_multipoles: bfloat16 [32, 32, 32, 2, 256], P('gx', 'gy'), may hold values from -6 to 6
- m2m_ops: bfloat16 [2, 2, 2, 256, 256], replicated, may hold values from -0.125 to 0.125
- m2l_ops: bfloat16 [512, 256, 256], P('gy'), may hold values from -0.015625 to 0.015625
- offsets: int32 [512, 3], P('gy'), may hold values from -7 to 7, as said below
Outputs:
- local_expansions: float32 [16, 256, 2, 256], P('gx', 'gy')
Inputs may be any that keep to these rules, and one draw needn't show every extreme that they name: Rows are distinct offsets; the first component lies in -3 to 3; in each row the largest magnitude of the three components is 2 or more.
All inputs are finite; a program needn't handle non-finite values.
Results may differ from a plain program's by a relative error of at most 0.0029.
Values may be sent and summed in bfloat16 or wider, within the bound.
A program may use at most 64 MiB of HBM per device.

v0:
```python
import jax
import jax.numpy as jnp
from jax import lax
from jax.sharding import PartitionSpec as P


def from_partner(array, axis, stride):
    return lax.ppermute(array, axis, [(i, i ^ 1 << stride) for i in range(lax.axis_size(axis))])


def passed_along(value, axis, steps):
    count = lax.axis_size(axis)
    pairs = [(source, (source + steps) % count) for source in range(count)]
    return lax.ppermute(value, axis, pairs)


def on_device(fine_multipoles, m2m_ops, m2l_ops, offsets):
    fine_boxes = fine_multipoles.shape[2]
    charge_sets = fine_multipoles.shape[3]
    coeffs = fine_multipoles.shape[4]
    half_z = fine_boxes // 2
    quarter = half_z // 2
    y_index = lax.axis_index("gy")
    parity = y_index % 2
    selected = lax.dynamic_index_in_dim(m2m_ops, parity, 1, keepdims=False)
    children = fine_multipoles[:, 0].reshape(2, half_z, 2, charge_sets, coeffs)
    partial_value = jnp.einsum(
        "azcri,acio->zro", children, selected, preferred_element_type=jnp.float32
    )
    kept_half = lax.dynamic_slice_in_dim(partial_value, parity * quarter, quarter, 0)
    sent_half = lax.dynamic_slice_in_dim(partial_value, (1 - parity) * quarter, quarter, 0)
    arrived = from_partner(sent_half, "gy", 0)
    coarse_mine = (kept_half + arrived).astype(jnp.bfloat16)
    slab_boxes = lax.all_gather(coarse_mine, "gy", axis=0, tiled=True)
    ahead_planes = [passed_along(slab_boxes, "gx", -distance) for distance in (1, 2, 3)]
    behind_planes = [passed_along(slab_boxes, "gx", distance) for distance in (1, 2, 3)]
    stacked = jnp.stack(behind_planes[::-1] + [slab_boxes] + ahead_planes)
    coarse_rows = slab_boxes.shape[0] // half_z
    plane_grid = stacked.reshape(7, coarse_rows, half_z, charge_sets, coeffs)
    count_ops = m2l_ops.shape[0]
    sources = []
    for op_entry in range(count_ops):
        shift_row = offsets[op_entry]
        chosen_plane = lax.dynamic_index_in_dim(plane_grid, shift_row[0] + 3, 0, keepdims=False)
        rolled = jnp.roll(chosen_plane, (-shift_row[1], -shift_row[2]), axis=(0, 1))
        sources.append(rolled.reshape(coarse_rows * half_z, charge_sets, coeffs))
    summed = jnp.zeros((quarter * lax.axis_size("gy") * charge_sets, coeffs), jnp.float32)
    for op_entry in range(count_ops):
        row_block = sources[op_entry].reshape(quarter * lax.axis_size("gy") * charge_sets, coeffs)
        summed = summed + jnp.dot(row_block, m2l_ops[op_entry], preferred_element_type=jnp.float32)
    my_locals = lax.psum_scatter(
        summed.reshape(quarter * lax.axis_size("gy"), charge_sets, coeffs),
        "gy",
        scatter_dimension=0,
        tiled=True,
    )
    return my_locals[None]


def solution(mesh):
    return jax.shard_map(
        on_device,
        mesh=mesh,
        in_specs=(P("gx", "gy", None, None, None), P(), P("gy", None, None), P("gy", None)),
        out_specs=P("gx", "gy", None, None),
        check_vma=False,
    )
```

profile of v0, /device:TPU:2, one launch (start us, length us, event | category | flops | bytes accessed | tf_op | source)
XLA Modules:
  0.0 762.5 jit_solution(14882671886684901363)
XLA Ops:
  6.5 1.2 copy-done
  7.8 1.0 convolution_bitcast_fusion
  8.8 3.5 collective-permute-start
  12.3 2.1 collective-permute-done
  14.5 127.3 %all_gather.3 = bf16[256,2,256]{2,0,1:T(8,128)(2,1)S(1)} all-gather(bf16[8,2,256]{2,0,1:T(8,128)(2,1)S(1)} %fusion.71), channel_id=1, replica_groups=mesh['gx'=16,'gy'=32] {'gy'}, dimensions={0}, use_global_device_ids=true | all-gather | bytes 270336 | tf_op jit(solution)/shard_map/all_gather | solution.py:34
  141.8 1.9 collective-permute-start.1
  143.7 2.1 fusion.73
  148.5 2.1 fusion.74
  163.8 8.3 %collective-permute-start.2 = (bf16[256,2,256]{2,0,1:T(8,128)(2,1)S(1)}, bf16[256,2,256]{2,0,1:T(8,128)(2,1)S(1)}, u32[]{:S(2)}, u32[]{:S(2)}) collective-permute-start(bf16[256,2,256]{2,0,1:T(8,128)(2,1)S(1)} %all_gather.3), channel_id=1, source_target_pairs={{0,64},{32,96},{64,128},{96,160},{128,192},{160,224},{192,256},{22... | collective-permute-start | bytes 786440 | tf_op jit(solution)/shard_map/ppermute | solution.py:14
  172.1 1.7 fusion.75
  183.4 3.3 collective-permute-start.3
  201.7 11.9 %collective-permute-start.4 = (bf16[256,2,256]{2,0,1:T(8,128)(2,1)S(1)}, bf16[256,2,256]{2,0,1:T(8,128)(2,1)S(1)}, u32[]{:S(2)}, u32[]{:S(2)}) collective-permute-start(bf16[256,2,256]{2,0,1:T(8,128)(2,1)S(1)} %all_gather.3), channel_id=1, source_target_pairs={{0,480},{32,0},{64,32},{96,64},{128,96},{160,128},{192,160},{224,1... | collective-permute-start | bytes 786440 | tf_op jit(solution)/shard_map/ppermute | solution.py:14
  213.6 6.3 collective-permute-start.5
  219.9 2.1 collective-permute-start.6
  222.1 1.9 collective-permute-done.4
  224.0 7.5 collective-permute-done.5
  231.5 4.8 collective-permute-done.6
  236.3 1.5 constant_dynamic-slice_fusion
  237.8 1.2 copy_bitcast_fusion
  239.7 0.7 fusion.4
  240.4 0.8 reshape_reshape.62
  241.2 2.3 copy_bitcast_fusion.2
  244.1 0.7 fusion.6
  244.9 0.8 reshape_reshape.61
  245.7 1.6 fusion.9
  247.3 0.7 fusion.8
  248.0 0.8 reshape_reshape.60
  248.8 2.3 copy_bitcast_fusion.4
  251.8 0.7 fusion.10
  252.5 0.8 reshape_reshape.59
  253.3 1.6 fusion.13
  255.0 0.7 fusion.12
  255.7 0.8 reshape_reshape.58
  256.5 2.3 copy_bitcast_fusion.6
  259.5 1.0 fusion.14
  260.4 0.8 reshape_reshape.57
  261.2 1.6 fusion.17
  262.8 0.7 fusion.16
  263.6 0.8 reshape_reshape.56
  264.4 1.3 copy_bitcast_fusion.8
  266.3 0.7 fusion.18
  267.1 0.8 reshape_reshape.55
  267.9 1.6 fusion.21
  269.5 0.7 fusion.20
  270.2 0.8 reshape_reshape.54
  273.0 0.8 reshape_reshape.53
  275.2 0.8 reshape_reshape.52
  278.0 0.8 reshape_reshape.51
  278.8 0.9 fusion.29
  280.5 0.8 reshape_reshape.50
  281.3 1.3 copy_bitcast_fusion.14
  283.9 0.8 reshape_reshape.49
  284.7 1.6 fusion.33
  286.4 1.5 fusion.32
  287.8 1.1 reshape_reshape.48
  288.9 1.6 fusion.3
  290.5 1.5 fusion.2
  292.0 1.8 reshape_reshape.63
  294.0 1.2 convolution_add_fusion.14
  299.4 1.1 convolution_add_fusion
  300.5 1.1 reshape.242
  301.6 1.3 dynamic-slice.8
  303.6 450.8 %all-reduce.3.cloned.1.call-done = f32[256,2,256]{2,1,0:T(2,128)} async-done(((f32[256,2,256]{2,1,0:T(2,128)}), f32[256,2,256]{2,1,0:T(2,128)}) %all-reduce.3.cloned.1.call-update) | async-done | bytes 524304
  754.3 1.3 dynamic-slice_bitcast_fusion
  (75 shorter events, 15.2 us)
Async XLA Ops:
  6.5 1.2 copy-start
  6.5 747.8 %all-reduce.3.cloned.1.call-start = ((), (), s32[]{:S(2)}) async-start(), calls=%async_computation | async-start | bytes 1048576
  8.8 5.6 collective-permute-start
  141.8 78.1 %collective-permute-start.1 = (bf16[256,2,256]{2,0,1:T(8,128)(2,1)S(1)}, bf16[256,2,256]{2,0,1:T(8,128)(2,1)S(1)}, u32[]{:S(2)}, u32[]{:S(2)}) collective-permute-start(bf16[256,2,256]{2,0,1:T(8,128)(2,1)S(1)} %all_gather.3), channel_id=1, source_target_pairs={{0,96},{32,128},{64,160},{96,192},{128,224},{160,256},{192,288},{2... | collective-permute-start | bytes 786440 | tf_op jit(solution)/shard_map/ppermute | solution.py:14
  163.8 58.2 %collective-permute-start.2 = (bf16[256,2,256]{2,0,1:T(8,128)(2,1)S(1)}, bf16[256,2,256]{2,0,1:T(8,128)(2,1)S(1)}, u32[]{:S(2)}, u32[]{:S(2)}) collective-permute-start(bf16[256,2,256]{2,0,1:T(8,128)(2,1)S(1)} %all_gather.3), channel_id=1, source_target_pairs={{0,64},{32,96},{64,128},{96,160},{128,192},{160,224},{192,256},{22... | collective-permute-start | bytes 786440 | tf_op jit(solution)/shard_map/ppermute | solution.py:14
  183.4 38.7 %collective-permute-start.3 = (bf16[256,2,256]{2,0,1:T(8,128)(2,1)S(1)}, bf16[256,2,256]{2,0,1:T(8,128)(2,1)S(1)}, u32[]{:S(2)}, u32[]{:S(2)}) collective-permute-start(bf16[256,2,256]{2,0,1:T(8,128)(2,1)S(1)} %all_gather.3), channel_id=1, source_target_pairs={{0,32},{32,64},{64,96},{96,128},{128,160},{160,192},{192,224},{224... | collective-permute-start | bytes 786440 | tf_op jit(solution)/shard_map/ppermute | solution.py:14
  201.7 22.3 %collective-permute-start.4 = (bf16[256,2,256]{2,0,1:T(8,128)(2,1)S(1)}, bf16[256,2,256]{2,0,1:T(8,128)(2,1)S(1)}, u32[]{:S(2)}, u32[]{:S(2)}) collective-permute-start(bf16[256,2,256]{2,0,1:T(8,128)(2,1)S(1)} %all_gather.3), channel_id=1, source_target_pairs={{0,480},{32,0},{64,32},{96,64},{128,96},{160,128},{192,160},{224,1... | collective-permute-start | bytes 786440 | tf_op jit(solution)/shard_map/ppermute | solution.py:14
  213.6 17.9 %collective-permute-start.5 = (bf16[256,2,256]{2,0,1:T(8,128)(2,1)S(1)}, bf16[256,2,256]{2,0,1:T(8,128)(2,1)S(1)}, u32[]{:S(2)}, u32[]{:S(2)}) collective-permute-start(bf16[256,2,256]{2,0,1:T(8,128)(2,1)S(1)} %all_gather.3), channel_id=1, source_target_pairs={{0,448},{32,480},{64,0},{96,32},{128,64},{160,96},{192,128},{224,1... | collective-permute-start | bytes 786440 | tf_op jit(solution)/shard_map/ppermute | solution.py:14
  219.9 16.4 %collective-permute-start.6 = (bf16[256,2,256]{2,0,1:T(8,128)(2,1)S(1)}, bf16[256,2,256]{2,0,1:T(8,128)(2,1)S(1)}, u32[]{:S(2)}, u32[]{:S(2)}) collective-permute-start(bf16[256,2,256]{2,0,1:T(8,128)(2,1)S(1)} %all_gather.3), channel_id=1, source_target_pairs={{0,416},{32,448},{64,480},{96,0},{128,32},{160,64},{192,96},{224,1... | collective-permute-start | bytes 786440 | tf_op jit(solution)/shard_map/ppermute | solution.py:14
  283.2 10.5 %copy-start.1 = (bf16[16,256,256]{2,1,0:T(8,128)(2,1)S(1)}, bf16[16,256,256]{2,1,0:T(8,128)(2,1)}, u32[]{:S(2)}) copy-start(bf16[16,256,256]{2,1,0:T(8,128)(2,1)} %param.8) | copy-start | bytes 6291460
  293.7 1.5 copy-start.15
  293.7 1.7 copy-start.13
  293.9 1.7 copy-start.12
  295.2 1.0 copy-start.11
  295.4 1.0 copy-start.10
  295.7 1.0 copy-start.9
  296.1 1.0 copy-start.8
  296.4 1.0 copy-start.7
  296.7 1.0 copy-start.6
  297.1 1.0 copy-start.5
  297.4 1.0 copy-start.4
  297.7 1.0 copy-start.3
  298.1 1.0 copy-start.2
  298.4 1.0 copy-start.14
Sparse Core Ops, SparseCore 0:
  301.8 452.5 all-reduce.2
where the time goes:
time: 764 us; the launch traced here: 762 us
  waiting for transfers between devices  467 us (61%)
  blocking collectives  127 us (17%)
  between operations  55 us (7%)
  local copies, waits for them, and re-layouts  39.3 us (5%)
  starting transfers between devices  37.2 us (5%)
  other arithmetic  30.1 us (4%)
    unnamed x2, waiting for transfers between devices  451 us
    all_gather x1, blocking collectives, on_device(): slab_boxes = lax.all_gather(coarse_mine, 'gy', axis=0, tiled=True)  127 us
    ppermute x6, starting transfers between devices, passed_along(): return lax.ppermute(value, axis, pairs)  33.7 us
    concatenate x32, other arithmetic, on_device(): rolled = jnp.roll(chosen_plane, (-shift_row[1], -shift_row[2]), axis=(0, 1))  30.1 us
  transfers between devices with their start and end apart: 8, of which 5 were waited for; matrix products, arithmetic and copies ran while one was open for 1% of the time, Pallas kernels for 0%

commit v1 on v0

--- a/solution.py
+++ b/solution.py
@@ -31,7 +31,9 @@
     sent_half = lax.dynamic_slice_in_dim(partial_value, (1 - parity) * quarter, quarter, 0)
     arrived = from_partner(sent_half, "gy", 0)
     coarse_mine = (kept_half + arrived).astype(jnp.bfloat16)
-    slab_boxes = lax.all_gather(coarse_mine, "gy", axis=0, tiled=True)
+    slab_boxes = jnp.concatenate(
+        lax.all_to_all(jnp.stack(lax.psum(1, "gy") * [coarse_mine], axis=0), "gy", 0, 0), axis=0
+    )
     ahead_planes = [passed_along(slab_boxes, "gx", -distance) for distance in (1, 2, 3)]
     behind_planes = [passed_along(slab_boxes, "gx", distance) for distance in (1, 2, 3)]
     stacked = jnp.stack(behind_planes[::-1] + [slab_boxes] + ahead_planes)

time: 764 us -> 709 us (0.928)
  blocking collectives: 127 us -> 33.5 us
  waiting for transfers between devices: 467 us -> 492 us
  other arithmetic: 30.1 us -> 41.6 us
    all_gather x1 -> x0, blocking collectives: 127 us -> none  [on_device(): slab_boxes = lax.all_gather(coarse_mine, 'gy', axis=0, tiled=True)]
    all_to_all x0 -> x1, blocking collectives: none -> 33.5 us  [on_device(): lax.all_to_all(jnp.stack(lax.psum(1, 'gy') * [coarse_mine], axis=0), 'gy'...]
    ppermute x6, waiting for transfers between devices: 14.1 us -> 38.9 us  [passed_along(): return lax.ppermute(value, axis, pairs)]
    concatenate x32 -> x24, other arithmetic: 30.1 us -> 41.5 us  [on_device(): rolled = jnp.roll(chosen_plane, (-shift_row[1], -shift_row[2]), axis=(0, 1))]
where the time goes in v1:
time: 709 us; the launch traced here: 707 us
  waiting for transfers between devices  492 us (69%)
  between operations  55.2 us (8%)
  other arithmetic  41.6 us (6%)
  starting transfers between devices  39.9 us (6%)
  local copies, waits for them, and re-layouts  38.2 us (5%)
  blocking collectives  33.5 us (5%)
    unnamed x2, waiting for transfers between devices  451 us
    concatenate x24, other arithmetic, on_device(): rolled = jnp.roll(chosen_plane, (-shift_row[1], -shift_row[2]), axis=(0, 1))  41.5 us
    ppermute x6, waiting for transfers between devices, passed_along(): return lax.ppermute(value, axis, pairs)  38.9 us
    ppermute x6, starting transfers between devices, passed_along(): return lax.ppermute(value, axis, pairs)  36.4 us
    all_to_all x1, blocking collectives, on_device(): lax.all_to_all(jnp.stack(lax.psum(1, 'gy') * [coarse_mine], axis=0), 'gy'...  33.5 us
    another operation x16, local copies, waits for them, and re-layouts, on_device(): sources[op_entry]  19.8 us
  transfers between devices with their start and end apart: 8, of which 5 were waited for; matrix products, arithmetic and copies ran while one was open for 1% of the time, Pallas kernels for 0%

profile of v1, /device:TPU:2, one launch (start us, length us, event | category | flops | bytes accessed | tf_op | source)
XLA Modules:
  0.0 707.1 jit_solution(1501902338324950360)
XLA Ops:
  6.5 1.2 copy-done
  7.8 1.0 convolution_bitcast_fusion
  8.8 3.5 collective-permute-start
  12.3 2.1 collective-permute-done
  14.6 33.5 %all_to_all.5 = bf16[32,8,2,256]{3,2,1,0:T(2,128)(2,1)S(1)} all-to-all(bf16[32,8,2,256]{3,2,1,0:T(2,128)(2,1)S(1)} %stack.18), channel_id=1, replica_groups=mesh['gx'=16,'gy'=32] {'gy'}, dimensions={0} | all-to-all | bytes 524288 | tf_op jit(solution)/shard_map/all_to_all | solution.py:35
  48.1 4.7 collective-permute-start.1
  52.8 2.1 fusion.73
  57.5 2.1 fusion.74
  73.2 7.3 %collective-permute-start.2 = (bf16[256,2,256]{2,1,0:T(2,128)(2,1)S(1)}, bf16[256,2,256]{2,1,0:T(2,128)(2,1)S(1)}, u32[]{:S(2)}, u32[]{:S(2)}) collective-permute-start(bf16[256,2,256]{2,1,0:T(2,128)(2,1)S(1)} %bitcast.255), channel_id=1, source_target_pairs={{0,64},{32,96},{64,128},{96,160},{128,192},{160,224},{192,256},{22... | collective-permute-start | bytes 786440 | tf_op jit(solution)/shard_map/ppermute | solution.py:14
  80.5 1.7 fusion.75
  91.8 1.9 collective-permute-start.3
  108.6 13.3 %collective-permute-start.4 = (bf16[256,2,256]{2,1,0:T(2,128)(2,1)S(1)}, bf16[256,2,256]{2,1,0:T(2,128)(2,1)S(1)}, u32[]{:S(2)}, u32[]{:S(2)}) collective-permute-start(bf16[256,2,256]{2,1,0:T(2,128)(2,1)S(1)} %bitcast.257), channel_id=1, source_target_pairs={{0,480},{32,0},{64,32},{96,64},{128,96},{160,128},{192,160},{224,1... | collective-permute-start | bytes 786440 | tf_op jit(solution)/shard_map/ppermute | solution.py:14
  121.9 7.3 %collective-permute-start.5 = (bf16[256,2,256]{2,1,0:T(2,128)(2,1)S(1)}, bf16[256,2,256]{2,1,0:T(2,128)(2,1)S(1)}, u32[]{:S(2)}, u32[]{:S(2)}) collective-permute-start(bf16[256,2,256]{2,1,0:T(2,128)(2,1)S(1)} %bitcast.258), channel_id=1, source_target_pairs={{0,448},{32,480},{64,0},{96,32},{128,64},{160,96},{192,128},{224,1... | collective-permute-start | bytes 786440 | tf_op jit(solution)/shard_map/ppermute | solution.py:14
  129.2 1.9 collective-permute-start.6
  132.1 2.9 collective-permute-done.4
  135.2 31.3 %collective-permute-done.5 = bf16[256,2,256]{2,1,0:T(2,128)(2,1)S(1)} collective-permute-done((bf16[256,2,256]{2,1,0:T(2,128)(2,1)S(1)}, bf16[256,2,256]{2,1,0:T(2,128)(2,1)S(1)}, u32[]{:S(2)}, u32[]{:S(2)}) %collective-permute-start.5) | collective-permute-done | bytes 262176 | tf_op jit(solution)/shard_map/ppermute | solution.py:14
  166.7 4.7 collective-permute-done.6
  171.6 4.8 dynamic-slice_bitcast_fusion
  176.4 2.0 fusion.3
  178.4 1.4 fusion.2
  179.8 1.7 reshape_reshape.63
  181.6 2.4 fusion.4
  184.0 1.7 reshape_reshape.62
  185.7 3.1 fusion.7
  188.8 1.4 fusion.6
  190.2 1.7 reshape_reshape.61
  192.0 2.4 fusion.8
  194.4 1.8 reshape_reshape.60
  196.1 3.1 fusion.11
  199.2 1.5 fusion.10
  200.7 1.8 reshape_reshape.59
  202.4 2.4 fusion.12
  204.8 1.8 reshape_reshape.58
  206.6 2.0 fusion.15
  208.6 0.7 fusion.14
  209.3 0.8 reshape_reshape.57
  210.1 1.9 fusion.16
  212.1 0.8 reshape_reshape.56
  212.9 1.3 fusion.19
  214.2 0.7 fusion.18
  214.9 0.8 reshape_reshape.55
  215.7 0.7 fusion.20
  216.5 0.8 reshape_reshape.54
  217.3 1.3 fusion.23
  218.6 0.7 fusion.22
  219.3 0.8 reshape_reshape.53
  220.1 0.7 fusion.24
  220.9 0.8 reshape_reshape.52
  221.7 2.0 fusion.27
  223.7 0.7 fusion.26
  224.4 0.8 reshape_reshape.51
  225.2 2.5 fusion.28
  227.8 1.7 reshape_reshape.50
  229.5 3.0 fusion.31
  232.5 1.0 fusion.30
  233.5 0.8 reshape_reshape.49
  234.3 2.4 fusion.32
  236.7 1.1 reshape_reshape.48
  238.0 1.2 convolution_add_fusion.14
  243.5 1.1 convolution_add_fusion
  244.6 1.1 reshape.248
  245.7 1.3 dynamic-slice.8
  247.7 451.3 %all-reduce.3.cloned.1.call-done = f32[256,2,256]{2,1,0:T(2,128)} async-done(((f32[256,2,256]{2,1,0:T(2,128)}), f32[256,2,256]{2,1,0:T(2,128)}) %all-reduce.3.cloned.1.call-update) | async-done | bytes 524304
  698.9 1.3 dynamic-slice_bitcast_fusion.16
  (61 shorter events, 6.1 us)
Async XLA Ops:
  6.5 1.2 copy-start
  6.5 692.4 %all-reduce.3.cloned.1.call-start = ((), (), s32[]{:S(2)}) async-start(), calls=%async_computation.1 | async-start | bytes 1048576
  8.8 5.6 collective-permute-start
  48.1 81.1 %collective-permute-start.1 = (bf16[256,2,256]{2,1,0:T(2,128)(2,1)S(1)}, bf16[256,2,256]{2,1,0:T(2,128)(2,1)S(1)}, u32[]{:S(2)}, u32[]{:S(2)}) collective-permute-start(bf16[256,2,256]{2,1,0:T(2,128)(2,1)S(1)} %bitcast.254), channel_id=1, source_target_pairs={{0,96},{32,128},{64,160},{96,192},{128,224},{160,256},{192,288},{2... | collective-permute-start | bytes 786440 | tf_op jit(solution)/shard_map/ppermute | solution.py:14
  73.2 58.1 %collective-permute-start.2 = (bf16[256,2,256]{2,1,0:T(2,128)(2,1)S(1)}, bf16[256,2,256]{2,1,0:T(2,128)(2,1)S(1)}, u32[]{:S(2)}, u32[]{:S(2)}) collective-permute-start(bf16[256,2,256]{2,1,0:T(2,128)(2,1)S(1)} %bitcast.255), channel_id=1, source_target_pairs={{0,64},{32,96},{64,128},{96,160},{128,192},{160,224},{192,256},{22... | collective-permute-start | bytes 786440 | tf_op jit(solution)/shard_map/ppermute | solution.py:14
  91.8 39.8 %collective-permute-start.3 = (bf16[256,2,256]{2,1,0:T(2,128)(2,1)S(1)}, bf16[256,2,256]{2,1,0:T(2,128)(2,1)S(1)}, u32[]{:S(2)}, u32[]{:S(2)}) collective-permute-start(bf16[256,2,256]{2,1,0:T(2,128)(2,1)S(1)} %bitcast.256), channel_id=1, source_target_pairs={{0,32},{32,64},{64,96},{96,128},{128,160},{160,192},{192,224},{224... | collective-permute-start | bytes 786440 | tf_op jit(solution)/shard_map/ppermute | solution.py:14
  108.6 26.3 %collective-permute-start.4 = (bf16[256,2,256]{2,1,0:T(2,128)(2,1)S(1)}, bf16[256,2,256]{2,1,0:T(2,128)(2,1)S(1)}, u32[]{:S(2)}, u32[]{:S(2)}) collective-permute-start(bf16[256,2,256]{2,1,0:T(2,128)(2,1)S(1)} %bitcast.257), channel_id=1, source_target_pairs={{0,480},{32,0},{64,32},{96,64},{128,96},{160,128},{192,160},{224,1... | collective-permute-start | bytes 786440 | tf_op jit(solution)/shard_map/ppermute | solution.py:14
  121.9 44.5 %collective-permute-start.5 = (bf16[256,2,256]{2,1,0:T(2,128)(2,1)S(1)}, bf16[256,2,256]{2,1,0:T(2,128)(2,1)S(1)}, u32[]{:S(2)}, u32[]{:S(2)}) collective-permute-start(bf16[256,2,256]{2,1,0:T(2,128)(2,1)S(1)} %bitcast.258), channel_id=1, source_target_pairs={{0,448},{32,480},{64,0},{96,32},{128,64},{160,96},{192,128},{224,1... | collective-permute-start | bytes 786440 | tf_op jit(solution)/shard_map/ppermute | solution.py:14
  129.2 42.2 %collective-permute-start.6 = (bf16[256,2,256]{2,1,0:T(2,128)(2,1)S(1)}, bf16[256,2,256]{2,1,0:T(2,128)(2,1)S(1)}, u32[]{:S(2)}, u32[]{:S(2)}) collective-permute-start(bf16[256,2,256]{2,1,0:T(2,128)(2,1)S(1)} %bitcast.259), channel_id=1, source_target_pairs={{0,416},{32,448},{64,480},{96,0},{128,32},{160,64},{192,96},{224,1... | collective-permute-start | bytes 786440 | tf_op jit(solution)/shard_map/ppermute | solution.py:14
  225.2 12.6 %copy-start.1 = (bf16[16,256,256]{2,1,0:T(8,128)(2,1)S(1)}, bf16[16,256,256]{2,1,0:T(8,128)(2,1)}, u32[]{:S(2)}) copy-start(bf16[16,256,256]{2,1,0:T(8,128)(2,1)} %param.8) | copy-start | bytes 6291460
  237.8 1.5 copy-start.15
  237.8 1.7 copy-start.14
  238.0 1.7 copy-start.13
  239.3 1.0 copy-start.12
  239.5 1.0 copy-start.11
  239.8 1.0 copy-start.10
  240.2 1.0 copy-start.9
  240.5 1.0 copy-start.8
  240.8 1.0 copy-start.7
  241.2 1.0 copy-start.6
  241.5 1.0 copy-start.5
  241.8 1.0 copy-start.4
  242.2 1.0 copy-start.3
  242.5 1.0 copy-start.2
Sparse Core Ops, SparseCore 0:
  245.8 453.0 all-reduce.2
